TPU v7x, 32 devices: a whole 2x2x4 slice. The times are simulated.
32 devices in a mesh: row: 8 (over y, x, core), col: 4 (over z).
Axes of the slice: x: 2, y: 2, z: 4, core: 2. Of those that a mesh axis runs over, the one named last changes fastest.
Arguments:
- tracers: float32 [40, 6, 64, 512], P(None, None, 'row', 'col'), may hold values from 0.1 to 10
- wind: float32 [2, 6, 64, 512], P(None, None, 'row', 'col'), may hold values from -2.4 to 2.4
- bin_shift: int32 [64, 512], P('row', 'col'), may hold values from 0 to 3
- shift_frac: float32 [64, 512], P('row', 'col'), may hold values from 0 to 1
Outputs:
- aerosol: float32 [40, 6, 64, 512], P(None, None, 'row', 'col')
All inputs are finite; a program needn't handle non-finite values.
Results may differ from a plain program's by a relative error of at most 0.0001.
Values sent between devices are 32-bit elements; how exact they have to be, the bound alone decides.
A program may use at most 64 MiB of HBM per device.

v0:
```python
import functools
import jax
import jax.numpy as jnp
import numpy as np
from jax import lax
from jax.experimental import pallas as pl
from jax.experimental.pallas import tpu as pltpu
from jax.sharding import PartitionSpec as P

step_size = 0.25
hyper_coef = 0.001
MESH = pl.DeviceIdType.MESH
CHUNKS = 3
PHASES = 4
LEFT, RIGHT, UP_LEFT, UP_RIGHT, DOWN_LEFT, DOWN_RIGHT = range(6)


def lobatto_derivative():
    points = np.array([-1.0, -1.0 / np.sqrt(5.0), 1.0 / np.sqrt(5.0), 1.0])
    weights = np.array(
        [1.0 / np.prod([points[j] - points[k] for k in range(4) if k != j]) for j in range(4)]
    )
    matrix = np.zeros((4, 4))
    for i in range(4):
        for j in range(4):
            if i != j:
                matrix[i, j] = weights[j] / weights[i] / (points[i] - points[j])
        matrix[i, i] = -np.sum(matrix[i])
    return matrix


DERIV = lobatto_derivative()
SECOND = DERIV @ DERIV


def seam_table(length):
    table = np.zeros((length + 128, length))
    for node in range(length):
        place = node % 4
        if place == 1 or place == 2:
            table[node, node] = 1.0
            continue
        table[node, node] = 0.5
        other = node + 1 if place == 3 else node - 1
        if 0 <= other < length:
            table[other, node] = 0.5
    for lane in (LEFT, UP_LEFT, DOWN_LEFT):
        table[length + lane, 0] = 0.5
    for lane in (RIGHT, UP_RIGHT, DOWN_RIGHT):
        table[length + lane, length - 1] = 0.5
    return table


def tables(length):
    first = np.kron(np.eye(length // 4), DERIV.T)
    second = first @ first
    seam = seam_table(length)
    hyper = -step_size * hyper_coef
    made = (
        np.concatenate([-step_size * first, second], axis=1),
        np.concatenate([hyper * (seam @ second), seam], axis=1),
        np.concatenate([seam, -step_size * (seam @ first), seam @ second], axis=1),
        seam,
    )
    return [jnp.asarray(m, dtype=jnp.float32) for m in made]


def parts(f):
    s = [f[0] + f[3], f[1] + f[2]]
    return s[0] - s[1], f[0] - f[3], f[1] - f[2]


def first_rows(split, scale):
    m = DERIV * (0.5 * scale)
    ss, d0, d1 = split
    out = [None] * 4
    for i in range(2):
        odd = float(m[i, 0] + m[i, 3]) * ss
        even = float(m[i, 0] - m[i, 3]) * d0 + float(m[i, 1] - m[i, 2]) * d1
        out[i], out[3 - i] = even + odd, even - odd
    return out


def second_rows(split, scale):
    m = SECOND * (0.5 * scale)
    ss, d0, d1 = split
    out = [None] * 4
    for i in range(2):
        even = float(m[i, 0] + m[i, 3]) * ss
        odd = float(m[i, 0] - m[i, 3]) * d0 + float(m[i, 1] - m[i, 2]) * d1
        out[i], out[3 - i] = even + odd, even - odd
    return out


def by_elements(fn, rows):
    out = []
    for start in range(0, len(rows), 4):
        out += fn(parts(rows[start : start + 4]))
    return out


def transport(
    sizes, tr, wind, m0, m1, m2, m3, out, held, ahead, row_out, row_in, edge_out, edge_in,
    row_send, row_recv, edge_send, edge_recv,
):
    bins, levels, nr, nc = sizes
    step = levels // CHUNKS
    flat = step * nr * bins
    row_n, col_n = lax.axis_size("row"), lax.axis_size("col")
    row, col = lax.axis_index("row"), lax.axis_index("col")
    up, down = lax.rem(row + row_n - 1, row_n), lax.rem(row + 1, row_n)
    left, right = lax.rem(col + col_n - 1, col_n), lax.rem(col + 1, col_n)
    partners = [
        (up, col), (down, col), (row, left), (row, right),
        (up, left), (up, right), (down, left), (down, right),
    ]
    barrier = pltpu.get_barrier_semaphore()
    for partner in partners:
        pl.semaphore_signal(barrier, inc=1, device_id=partner, device_id_type=MESH)

    def copies(phase, chunk):
        slot = phase * CHUNKS + chunk
        made = []
        for side, partner in ((0, (up, col)), (1, (down, col))):
            made.append(pltpu.make_async_remote_copy(
                src_ref=row_out.at[slot, side], dst_ref=row_in.at[slot, 1 - side],
                send_sem=row_send.at[slot, side], recv_sem=row_recv.at[slot, 1 - side],
                device_id=partner, device_id_type=MESH,
            ))
        for side, lane, partner in (
            (0, RIGHT, (row, left)), (1, LEFT, (row, right)),
            (0, DOWN_RIGHT, (up, left)), (0, UP_RIGHT, (down, left)),
            (1, DOWN_LEFT, (up, right)), (1, UP_LEFT, (down, right)),
        ):
            made.append(pltpu.make_async_remote_copy(
                src_ref=edge_out.at[slot, side], dst_ref=edge_in.at[slot, lane],
                send_sem=edge_send.at[slot, lane], recv_sem=edge_recv.at[slot, lane],
                device_id=partner, device_id_type=MESH,
            ))
        return made

    def as_rows(field):
        shaped = field.reshape(step, nr, bins, nc)
        return [shaped[:, r] for r in range(nr)]

    def flatten(rows):
        return jnp.stack(rows, axis=1).reshape(flat, nc)

    def times(field, table):
        return jnp.dot(
            field, table[...], precision=lax.Precision.HIGHEST,
            preferred_element_type=jnp.float32,
        )

    def send(phase, chunk, rows):
        slot = phase * CHUNKS + chunk
        row_out[slot, 0] = rows[0]
        row_out[slot, 1] = rows[nr - 1]
        for r in range(nr):
            held[chunk, r] = rows[r]
        turned = flatten(rows).T
        edge_out[slot, 0] = turned[0:1]
        edge_out[slot, 1] = turned[nc - 1 : nc]
        if phase == 0 and chunk == 0:
            pl.semaphore_wait(barrier, len(partners))
        for copy in copies(phase, chunk):
            copy.start()

    def row_seam(rows, above, below):
        done = list(rows)
        for r in range(3, nr - 1, 4):
            done[r] = done[r + 1] = 0.5 * rows[r] + 0.5 * rows[r + 1]
        done[0] = 0.5 * rows[0] + 0.5 * above
        done[nr - 1] = 0.5 * rows[nr - 1] + 0.5 * below
        return done

    def joined(phase, chunk):
        slot = phase * CHUNKS + chunk
        for copy in copies(phase, chunk):
            copy.wait_recv()
        rows = row_seam([held[chunk, r] for r in range(nr)], row_in[slot, 0], row_in[slot, 1])
        lanes = jnp.concatenate(
            [edge_in[slot, i] for i in range(6)] + [jnp.zeros((122, flat), jnp.float32)], axis=0
        )
        edges = as_rows(lanes.T)
        lane = lax.broadcasted_iota(jnp.int32, edges[0].shape, 2)
        own = lane < 2
        side = [jnp.where(own, e, 0.0) for e in edges]
        from_up = jnp.where((lane >= 2) & (lane < 4), edges[nr - 1], 0.0)
        from_down = jnp.where((lane >= 4) & (lane < 6), edges[0], 0.0)
        side = row_seam(side, from_up, from_down)
        return jnp.concatenate([flatten(rows), flatten(side)], axis=1)

    def wind_rows(chunk, which):
        return [
            wind[which, chunk * step : (chunk + 1) * step, r : r + 1, :] for r in range(nr)
        ]

    def tracer_rows(chunk):
        rows = []
        for r in range(nr):
            pieces = [
                tr[pl.ds((chunk * step + l) * nr + r, bins, stride=levels * nr), :]
                for l in range(step)
            ]
            rows.append(jnp.stack(pieces, axis=0))
        return rows

    def lead(chunk, rows, slope_x, second_x, start, scale):
        wx, wy = wind_rows(chunk, 0), wind_rows(chunk, 1)
        slope_y = by_elements(lambda s: first_rows(s, -step_size), rows)
        second_y = by_elements(lambda s: second_rows(s, 1.0), rows)
        sx, lx = as_rows(slope_x), as_rows(second_x)
        laplace = []
        for r in range(nr):
            moved = rows[r] + wx[r] * sx[r] + wy[r] * slope_y[r]
            if start is not None:
                moved = scale * start[r] + scale * moved
            ahead[chunk, r] = moved
            laplace.append(lx[r] + second_y[r])
        return laplace

    def finish(chunk, made, scale):
        hx, h = as_rows(made[:, :nc]), as_rows(made[:, nc:])
        hy = by_elements(lambda s: second_rows(s, -step_size * hyper_coef), h)
        return [ahead[chunk, r] + scale * (hx[r] + hy[r]) for r in range(nr)]

    for chunk in range(CHUNKS):
        rows = tracer_rows(chunk)
        made = times(flatten(rows), m0)
        send(0, chunk, lead(chunk, rows, made[:, :nc], made[:, nc:], None, 1.0))
    for chunk in range(CHUNKS):
        send(1, chunk, finish(chunk, times(joined(0, chunk), m1), 1.0))
    for chunk in range(CHUNKS):
        made = times(joined(1, chunk), m2)
        rows = as_rows(made[:, :nc])
        send(2, chunk, lead(
            chunk, rows, made[:, nc : 2 * nc], made[:, 2 * nc :], tracer_rows(chunk), 0.5
        ))
    for chunk in range(CHUNKS):
        send(3, chunk, finish(chunk, times(joined(2, chunk), m1), 0.5))
    for chunk in range(CHUNKS):
        rows = as_rows(times(joined(3, chunk), m3))
        for r in range(nr):
            for l in range(step):
                out[pl.ds((chunk * step + l) * nr + r, bins, stride=levels * nr), :] = rows[r][l]
    for phase in range(PHASES):
        for chunk in range(CHUNKS):
            for copy in copies(phase, chunk):
                copy.wait_send()


def remap(sizes, field, shift, frac, out):
    bins, levels, nr, nc = sizes
    weights = []
    for amount in range(5):
        weights.append(
            jnp.where(shift[...] == amount, 1.0 - frac[...], 0.0)
            + jnp.where(shift[...] + 1 == amount, frac[...], 0.0)
        )
    for level in range(levels):
        for b in range(bins - 1):
            total = weights[0] * field[b, level]
            for k in range(1, min(b, 4) + 1):
                total = total + weights[k] * field[b - k, level]
            out[b, level] = total
        top = field[bins - 1, level]
        total = weights[0] * top
        for k in range(1, 5):
            top = top + field[bins - 1 - k, level]
            total = total + weights[k] * top
        out[bins - 1, level] = total


def body(tracers, wind, bin_shift, shift_frac):
    sizes = tracers.shape
    bins, levels, nr, nc = sizes
    step = levels // CHUNKS
    flat = step * nr * bins
    slots = PHASES * CHUNKS
    vmem = pl.BlockSpec(memory_space=pltpu.VMEM)
    field = pl.pallas_call(
        functools.partial(transport, sizes),
        out_shape=jax.ShapeDtypeStruct((bins * levels * nr, nc), jnp.float32),
        in_specs=[vmem] * 6,
        out_specs=vmem,
        scratch_shapes=[
            pltpu.VMEM((CHUNKS, nr, step, bins, nc), jnp.float32),
            pltpu.VMEM((CHUNKS, nr, step, bins, nc), jnp.float32),
            pltpu.VMEM((slots, 2, step, bins, nc), jnp.float32),
            pltpu.VMEM((slots, 2, step, bins, nc), jnp.float32),
            pltpu.VMEM((slots, 2, 1, flat), jnp.float32),
            pltpu.VMEM((slots, 6, 1, flat), jnp.float32),
            pltpu.SemaphoreType.DMA((slots, 2)),
            pltpu.SemaphoreType.DMA((slots, 2)),
            pltpu.SemaphoreType.DMA((slots, 6)),
            pltpu.SemaphoreType.DMA((slots, 6)),
        ],
        compiler_params=pltpu.CompilerParams(
            collective_id=0, has_side_effects=True, vmem_limit_bytes=40 << 20
        ),
        name="transport",
    )(tracers.reshape(bins * levels * nr, nc), wind, *tables(nc))
    return pl.pallas_call(
        functools.partial(remap, sizes),
        out_shape=jax.ShapeDtypeStruct(sizes, jnp.float32),
        in_specs=[vmem] * 3,
        out_specs=vmem,
        name="remap",
    )(field.reshape(sizes), bin_shift, shift_frac)


def solution(mesh):
    placed = (
        P(None, None, "row", "col"),
        P(None, None, "row", "col"),
        P("row", "col"),
        P("row", "col"),
    )
    return jax.shard_map(
        body, mesh=mesh, in_specs=placed, out_specs=P(None, None, "row", "col"), check_vma=False
    )
```

profile of v0, /device:TPU:0, one launch (start us, length us, event | category | flops | bytes accessed | tf_op | source)
XLA Modules:
  0.0 42.2 jit_solution(3222250011666360065)
XLA Ops:
  0.0 0.0 copy-start.1
  0.0 1.2 %copy-done.1 = f32[40,6,8,128]{3,2,1,0:T(8,128)S(1)} copy-done((f32[40,6,8,128]{3,2,1,0:T(8,128)S(1)}, f32[40,6,8,128]{3,2,1,0:T(8,128)}, u32[]{:S(2)}) %copy-start.1) | copy-done | bytes 983064
  1.2 0.0 copy-start.2
  1.2 1.0 %copy-done.2 = f32[256,384]{1,0:T(8,128)S(1)} copy-done((f32[256,384]{1,0:T(8,128)S(1)}, f32[256,384]{1,0:T(8,128)}, u32[]{:S(2)}) %copy-start.2) | copy-done | bytes 393240
  2.2 0.0 copy-start.3
  2.2 0.9 %copy-done.3 = f32[256,256]{1,0:T(8,128)S(1)} copy-done((f32[256,256]{1,0:T(8,128)S(1)}, f32[256,256]{1,0:T(8,128)}, u32[]{:S(2)}) %copy-start.3) | copy-done | bytes 262168
  3.1 0.0 copy-start.4
  3.2 0.9 %copy-done.4 = f32[256,128]{1,0:T(8,128)S(1)} copy-done((f32[256,128]{1,0:T(8,128)S(1)}, f32[256,128]{1,0:T(8,128)}, u32[]{:S(2)}) %copy-start.4) | copy-done | bytes 131096
  4.1 0.0 copy-start.5
  4.1 0.9 %copy-done.5 = f32[128,256]{1,0:T(8,128)S(1)} copy-done((f32[128,256]{1,0:T(8,128)S(1)}, f32[128,256]{1,0:T(8,128)}, u32[]{:S(2)}) %copy-start.5) | copy-done | bytes 131096
  5.0 0.0 copy-start.6
  5.0 0.8 %copy-done.6 = f32[2,6,8,128]{3,2,1,0:T(8,128)S(1)} copy-done((f32[2,6,8,128]{3,2,1,0:T(8,128)S(1)}, f32[2,6,8,128]{3,2,1,0:T(8,128)}, u32[]{:S(2)}) %copy-start.6) | copy-done | bytes 49176
  5.8 33.1 %transport.1 = f32[1920,128]{1,0:T(8,128)S(1)} custom-call(f32[1920,128]{1,0:T(8,128)S(1)} %bitcast.3, f32[2,6,8,128]{3,2,1,0:T(8,128)S(1)} %copy-done.6, f32[128,256]{1,0:T(8,128)S(1)} %copy-done.5, f32[256,256]{1,0:T(8,128)S(1)} %copy-done.3, f32[256,384]{1,0:T(8,128)S(1)} %copy-done.2, f32[256,128]{1,0:T(8,128)S(1)} %copy-done.4), custom_call_target="tpu_custom_call" | custom-call | tf_op jit(solution)/shard_map/transport/pallas_call | solution.py:282
  38.8 0.0 copy-start
  38.8 0.9 %copy-done = f32[1920,128]{1,0:T(8,128)} copy-done((f32[1920,128]{1,0:T(8,128)}, f32[1920,128]{1,0:T(8,128)S(1)}, u32[]{:S(2)}) %copy-start) | copy-done | bytes 983064
  39.8 2.4 %remap.1 = f32[40,6,8,128]{3,2,1,0:T(8,128)} custom-call(f32[40,6,8,128]{3,2,1,0:T(8,128)} %bitcast.2, s32[8,128]{1,0:T(8,128)} %shift.1, f32[8,128]{1,0:T(8,128)} %frac.1), custom_call_target="tpu_custom_call" | custom-call | tf_op jit(solution)/shard_map/remap/pallas_call | solution.py:304
Async XLA Ops:
  0.0 1.2 %copy-start.1 = (f32[40,6,8,128]{3,2,1,0:T(8,128)S(1)}, f32[40,6,8,128]{3,2,1,0:T(8,128)}, u32[]{:S(2)}) copy-start(f32[40,6,8,128]{3,2,1,0:T(8,128)} %param.8) | copy-start | bytes 2949124
  1.2 1.0 %copy-start.2 = (f32[256,384]{1,0:T(8,128)S(1)}, f32[256,384]{1,0:T(8,128)}, u32[]{:S(2)}) copy-start(f32[256,384]{1,0:T(8,128)} %constant.10.clone.m2) | copy-start | bytes 1179652
  2.2 0.9 %copy-start.3 = (f32[256,256]{1,0:T(8,128)S(1)}, f32[256,256]{1,0:T(8,128)}, u32[]{:S(2)}) copy-start(f32[256,256]{1,0:T(8,128)} %constant.9.clone.m1) | copy-start | bytes 786436
  3.1 0.9 %copy-start.4 = (f32[256,128]{1,0:T(8,128)S(1)}, f32[256,128]{1,0:T(8,128)}, u32[]{:S(2)}) copy-start(f32[256,128]{1,0:T(8,128)} %constant.11.clone.m3) | copy-start | bytes 393220
  4.1 0.9 %copy-start.5 = (f32[128,256]{1,0:T(8,128)S(1)}, f32[128,256]{1,0:T(8,128)}, u32[]{:S(2)}) copy-start(f32[128,256]{1,0:T(8,128)} %constant.8.clone.m0) | copy-start | bytes 393220
  5.0 0.8 %copy-start.6 = (f32[2,6,8,128]{3,2,1,0:T(8,128)S(1)}, f32[2,6,8,128]{3,2,1,0:T(8,128)}, u32[]{:S(2)}) copy-start(f32[2,6,8,128]{3,2,1,0:T(8,128)} %wind.1) | copy-start | bytes 147460
  38.8 1.0 %copy-start = (f32[1920,128]{1,0:T(8,128)}, f32[1920,128]{1,0:T(8,128)S(1)}, u32[]{:S(2)}) copy-start(f32[1920,128]{1,0:T(8,128)S(1)} %transport.1) | copy-start | bytes 2949124
where the time goes:
time: 42.6 us; the launch traced here: 42.2 us
  Pallas kernels  35.5 us (83%)
  local copies, waits for them, and re-layouts  6.7 us (16%)
    pallas_call x1, Pallas kernels, body(): pl.pallas_call(functools.partial(transport, sizes), out_shape=jax.ShapeDt...  33.1 us
    unnamed x14, local copies, waits for them, and re-layouts  6.7 us
    pallas_call x1, Pallas kernels, body(): pl.pallas_call(functools.partial(remap, sizes), out_shape=jax.ShapeDtypeS...  2.44 us

commit v1 on v0

--- a/solution.py
+++ b/solution.py
@@ -10,8 +10,9 @@
 step_size = 0.25
 hyper_coef = 0.001
 MESH = pl.DeviceIdType.MESH
-CHUNKS = 3
+CHUNKS = 2
 PHASES = 4
+COMM = True
 LEFT, RIGHT, UP_LEFT, UP_RIGHT, DOWN_LEFT, DOWN_RIGHT = range(6)
 
 
@@ -59,10 +60,22 @@
     made = (
         np.concatenate([-step_size * first, second], axis=1),
         np.concatenate([hyper * (seam @ second), seam], axis=1),
-        np.concatenate([seam, -step_size * (seam @ first), seam @ second], axis=1),
+        np.concatenate([-step_size * (seam @ first), seam @ second, seam], axis=1),
         seam,
     )
-    return [jnp.asarray(m, dtype=jnp.float32) for m in made]
+    return [m.astype(np.float32) for m in made]
+
+
+def split_tables(length):
+    high = [m.astype(jnp.bfloat16) for m in tables(length)]
+    low = [
+        (m - h.astype(np.float32)).astype(jnp.bfloat16) for m, h in zip(tables(length), high)
+    ]
+    opening = np.concatenate([high[0], low[0]], axis=1)
+    rest = np.concatenate(
+        [high[1], low[1][:, :length], high[2], low[2][:, : 2 * length], high[3]], axis=1
+    )
+    return [jnp.asarray(opening), jnp.asarray(rest)]
 
 
 def parts(f):
@@ -100,8 +113,9 @@
 
 
 def transport(
-    sizes, tr, wind, m0, m1, m2, m3, out, held, ahead, row_out, row_in, edge_out, edge_in,
-    row_send, row_recv, edge_send, edge_recv,
+    sizes, tr_in, wind_in, shift_in, frac_in, opening_in, rest_in, out, field, wind, shift, frac,
+    opening, rest, moved_on, held, ahead, row_out, row_in, edge_out, edge_in,
+    row_send, row_recv, edge_send, edge_recv, tr_sem, in_sem,
 ):
     bins, levels, nr, nc = sizes
     step = levels // CHUNKS
@@ -114,6 +128,25 @@
         (up, col), (down, col), (row, left), (row, right),
         (up, left), (up, right), (down, left), (down, right),
     ]
+    tr = field.reshape(bins * levels * nr, nc)
+    tr_loads = []
+    for chunk in range(CHUNKS):
+        part = pl.ds(chunk * step, step)
+        tr_loads.append(
+            pltpu.make_async_copy(tr_in.at[:, part], field.at[:, part], tr_sem.at[chunk])
+        )
+    loads = [
+        pltpu.make_async_copy(source, target, in_sem.at[i])
+        for i, (source, target) in enumerate((
+            (opening_in, opening), (wind_in, wind), (rest_in, rest), (shift_in, shift),
+            (frac_in, frac),
+        ))
+    ]
+    tr_loads[0].start()
+    for load in loads[:2]:
+        load.start()
+    for load in tr_loads[1:] + loads[2:]:
+        load.start()
     barrier = pltpu.get_barrier_semaphore()
     for partner in partners:
         pl.semaphore_signal(barrier, inc=1, device_id=partner, device_id_type=MESH)
@@ -146,11 +179,34 @@
     def flatten(rows):
         return jnp.stack(rows, axis=1).reshape(flat, nc)
 
-    def times(field, table):
-        return jnp.dot(
-            field, table[...], precision=lax.Precision.HIGHEST,
-            preferred_element_type=jnp.float32,
-        )
+    def times(field, table, at, wide, low_at, low_wide):
+        def dot(lhs, start, width):
+            return jnp.dot(
+                lhs, table[: lhs.shape[1], start : start + width],
+                preferred_element_type=jnp.float32,
+            )
+
+        high = field.astype(jnp.bfloat16)
+        low = (field - high.astype(jnp.float32)).astype(jnp.bfloat16)
+        total = dot(high, at, wide) + dot(low, at, wide)
+        cols = [total[:, i : i + nc] for i in range(0, wide, nc)]
+        if low_wide:
+            more = dot(high, low_at, low_wide)
+            for i in range(low_wide // nc):
+                cols[i] = cols[i] + more[:, i * nc : (i + 1) * nc]
+        return [as_rows(c) for c in cols]
+
+    def first_table(field):
+        return times(field, opening, 0, 2 * nc, 2 * nc, 2 * nc)
+
+    def hyper_table(field):
+        return times(field, rest, 0, 2 * nc, 2 * nc, nc)
+
+    def middle_table(field):
+        return times(field, rest, 3 * nc, 3 * nc, 6 * nc, 2 * nc)
+
+    def last_table(field):
+        return times(field, rest, 8 * nc, nc, 0, 0)[0]
 
     def send(phase, chunk, rows):
         slot = phase * CHUNKS + chunk
@@ -161,6 +217,8 @@
         turned = flatten(rows).T
         edge_out[slot, 0] = turned[0:1]
         edge_out[slot, 1] = turned[nc - 1 : nc]
+        if not COMM:
+            return
         if phase == 0 and chunk == 0:
             pl.semaphore_wait(barrier, len(partners))
         for copy in copies(phase, chunk):
@@ -176,7 +234,7 @@
 
     def joined(phase, chunk):
         slot = phase * CHUNKS + chunk
-        for copy in copies(phase, chunk):
+        for copy in copies(phase, chunk) if COMM else ():
             copy.wait_recv()
         rows = row_seam([held[chunk, r] for r in range(nr)], row_in[slot, 0], row_in[slot, 1])
         lanes = jnp.concatenate(
@@ -210,7 +268,7 @@
         wx, wy = wind_rows(chunk, 0), wind_rows(chunk, 1)
         slope_y = by_elements(lambda s: first_rows(s, -step_size), rows)
         second_y = by_elements(lambda s: second_rows(s, 1.0), rows)
-        sx, lx = as_rows(slope_x), as_rows(second_x)
+        sx, lx = slope_x, second_x
         laplace = []
         for r in range(nr):
             moved = rows[r] + wx[r] * sx[r] + wy[r] * slope_y[r]
@@ -221,55 +279,59 @@
         return laplace
 
     def finish(chunk, made, scale):
-        hx, h = as_rows(made[:, :nc]), as_rows(made[:, nc:])
+        hx, h = made
         hy = by_elements(lambda s: second_rows(s, -step_size * hyper_coef), h)
         return [ahead[chunk, r] + scale * (hx[r] + hy[r]) for r in range(nr)]
 
-    for chunk in range(CHUNKS):
+    def remap(weights, level):
+        def at(b):
+            return moved_on[(b * levels + level) * nr : (b * levels + level + 1) * nr, :]
+
+        for b in range(bins - 1):
+            total = weights[0] * at(b)
+            for k in range(1, min(b, 4) + 1):
+                total = total + weights[k] * at(b - k)
+            out[b, level] = total
+        top = at(bins - 1)
+        total = weights[0] * top
+        for k in range(1, 5):
+            top = top + at(bins - 1 - k)
+            total = total + weights[k] * top
+        out[bins - 1, level] = total
+
+    for chunk in range(CHUNKS):
+        tr_loads[chunk].wait()
+        if chunk == 0:
+            loads[0].wait()
+            loads[1].wait()
         rows = tracer_rows(chunk)
-        made = times(flatten(rows), m0)
-        send(0, chunk, lead(chunk, rows, made[:, :nc], made[:, nc:], None, 1.0))
-    for chunk in range(CHUNKS):
-        send(1, chunk, finish(chunk, times(joined(0, chunk), m1), 1.0))
-    for chunk in range(CHUNKS):
-        made = times(joined(1, chunk), m2)
-        rows = as_rows(made[:, :nc])
-        send(2, chunk, lead(
-            chunk, rows, made[:, nc : 2 * nc], made[:, 2 * nc :], tracer_rows(chunk), 0.5
-        ))
-    for chunk in range(CHUNKS):
-        send(3, chunk, finish(chunk, times(joined(2, chunk), m1), 0.5))
-    for chunk in range(CHUNKS):
-        rows = as_rows(times(joined(3, chunk), m3))
-        for r in range(nr):
-            for l in range(step):
-                out[pl.ds((chunk * step + l) * nr + r, bins, stride=levels * nr), :] = rows[r][l]
-    for phase in range(PHASES):
+        send(0, chunk, lead(chunk, rows, *first_table(flatten(rows)), None, 1.0))
+    for load in loads[2:]:
+        load.wait()
+    for chunk in range(CHUNKS):
+        send(1, chunk, finish(chunk, hyper_table(joined(0, chunk)), 1.0))
+    for chunk in range(CHUNKS):
+        slope_x, second_x, rows = middle_table(joined(1, chunk))
+        send(2, chunk, lead(chunk, rows, slope_x, second_x, tracer_rows(chunk), 0.5))
+    for chunk in range(CHUNKS):
+        send(3, chunk, finish(chunk, hyper_table(joined(2, chunk)), 0.5))
+    weights = []
+    for k in range(5):
+        weights.append(
+            jnp.where(shift[...] == k, 1.0 - frac[...], 0.0)
+            + jnp.where(shift[...] + 1 == k, frac[...], 0.0)
+        )
+    for chunk in range(CHUNKS):
+        rows = last_table(joined(3, chunk))
+        for l in range(step):
+            level = chunk * step + l
+            for r in range(nr):
+                moved_on[pl.ds(level * nr + r, bins, stride=levels * nr), :] = rows[r][l]
+            remap(weights, level)
+    for phase in range(PHASES if COMM else 0):
         for chunk in range(CHUNKS):
             for copy in copies(phase, chunk):
                 copy.wait_send()
-
-
-def remap(sizes, field, shift, frac, out):
-    bins, levels, nr, nc = sizes
-    weights = []
-    for amount in range(5):
-        weights.append(
-            jnp.where(shift[...] == amount, 1.0 - frac[...], 0.0)
-            + jnp.where(shift[...] + 1 == amount, frac[...], 0.0)
-        )
-    for level in range(levels):
-        for b in range(bins - 1):
-            total = weights[0] * field[b, level]
-            for k in range(1, min(b, 4) + 1):
-                total = total + weights[k] * field[b - k, level]
-            out[b, level] = total
-        top = field[bins - 1, level]
-        total = weights[0] * top
-        for k in range(1, 5):
-            top = top + field[bins - 1 - k, level]
-            total = total + weights[k] * top
-        out[bins - 1, level] = total
 
 
 def body(tracers, wind, bin_shift, shift_frac):
@@ -278,13 +340,20 @@
     step = levels // CHUNKS
     flat = step * nr * bins
     slots = PHASES * CHUNKS
-    vmem = pl.BlockSpec(memory_space=pltpu.VMEM)
-    field = pl.pallas_call(
+    opening, rest = split_tables(nc)
+    return pl.pallas_call(
         functools.partial(transport, sizes),
-        out_shape=jax.ShapeDtypeStruct((bins * levels * nr, nc), jnp.float32),
-        in_specs=[vmem] * 6,
-        out_specs=vmem,
+        out_shape=jax.ShapeDtypeStruct(sizes, jnp.float32),
+        in_specs=[pl.BlockSpec(memory_space=pltpu.HBM)] * 6,
+        out_specs=pl.BlockSpec(memory_space=pltpu.VMEM),
         scratch_shapes=[
+            pltpu.VMEM(sizes, jnp.float32),
+            pltpu.VMEM(wind.shape, jnp.float32),
+            pltpu.VMEM(bin_shift.shape, jnp.int32),
+            pltpu.VMEM(shift_frac.shape, jnp.float32),
+            pltpu.VMEM(opening.shape, jnp.bfloat16),
+            pltpu.VMEM(rest.shape, jnp.bfloat16),
+            pltpu.VMEM((bins * levels * nr, nc), jnp.float32),
             pltpu.VMEM((CHUNKS, nr, step, bins, nc), jnp.float32),
             pltpu.VMEM((CHUNKS, nr, step, bins, nc), jnp.float32),
             pltpu.VMEM((slots, 2, step, bins, nc), jnp.float32),
@@ -295,19 +364,14 @@
             pltpu.SemaphoreType.DMA((slots, 2)),
             pltpu.SemaphoreType.DMA((slots, 6)),
             pltpu.SemaphoreType.DMA((slots, 6)),
+            pltpu.SemaphoreType.DMA((CHUNKS,)),
+            pltpu.SemaphoreType.DMA((5,)),
         ],
         compiler_params=pltpu.CompilerParams(
-            collective_id=0, has_side_effects=True, vmem_limit_bytes=40 << 20
+            collective_id=0, has_side_effects=True, vmem_limit_bytes=63 << 20
         ),
         name="transport",
-    )(tracers.reshape(bins * levels * nr, nc), wind, *tables(nc))
-    return pl.pallas_call(
-        functools.partial(remap, sizes),
-        out_shape=jax.ShapeDtypeStruct(sizes, jnp.float32),
-        in_specs=[vmem] * 3,
-        out_specs=vmem,
-        name="remap",
-    )(field.reshape(sizes), bin_shift, shift_frac)
+    )(tracers, wind, bin_shift, shift_frac, opening, rest)
 
 
 def solution(mesh):

time: 42.6 us -> 32.9 us (0.77)
  Pallas kernels: 35.5 us -> 30.5 us
  local copies, waits for them, and re-layouts: 6.7 us -> 2.21 us
    unnamed x14 -> x1, local copies, waits for them, and re-layouts: 6.7 us -> 2.21 us
    pallas_call x1, Pallas kernels: 33.1 us -> 30.5 us  [body(): pl.pallas_call(functools.partial(transport, sizes), out_shape=jax.ShapeDt...]
    pallas_call x1 -> x0, Pallas kernels: 2.44 us -> none  [body(): pl.pallas_call(functools.partial(remap, sizes), out_shape=jax.ShapeDtypeS...]
where the time goes in v1:
time: 32.9 us; the launch traced here: 32.7 us
  Pallas kernels  30.5 us (93%)
  local copies, waits for them, and re-layouts  2.21 us (7%)
    pallas_call x1, Pallas kernels, body(): pl.pallas_call(functools.partial(transport, sizes), out_shape=jax.ShapeDt...  30.5 us
    unnamed x1, local copies, waits for them, and re-layouts  2.21 us

profile of v1, /device:TPU:0, one launch (start us, length us, event | category | flops | bytes accessed | tf_op | source)
XLA Modules:
  0.0 32.7 jit_solution(16482160721533942079)
XLA Ops:
  0.0 30.5 %transport.1 = f32[40,6,8,128]{3,2,1,0:T(8,128)} custom-call(f32[40,6,8,128]{3,2,1,0:T(8,128)} %tr_in.1, f32[2,6,8,128]{3,2,1,0:T(8,128)} %wind_in.1, s32[8,128]{1,0:T(8,128)} %shift_in.1, f32[8,128]{1,0:T(8,128)} %frac_in.1, bf16[128,512]{1,0:T(8,128)(2,1)} %constant.4.clone.opening_in, bf16[256,1152]{1,0:T(8,128)(2,1)} %constant.5.clone.rest_in), custom_call_target="tpu_custom_call" | custom-call | tf_op jit(solution)/shard_map/transport/pallas_call | solution.py:344
  30.5 2.2 %copy.8 = f32[40,6,8,128]{3,2,1,0:T(8,128)} copy(f32[40,6,8,128]{3,2,1,0:T(8,128)} %transport.1) | data formatting | bytes 1966080

commit v2 on v1

--- a/solution.py
+++ b/solution.py
@@ -11,7 +11,7 @@
 hyper_coef = 0.001
 MESH = pl.DeviceIdType.MESH
 CHUNKS = 2
-PHASES = 4
+PHASES = 2
 COMM = True
 LEFT, RIGHT, UP_LEFT, UP_RIGHT, DOWN_LEFT, DOWN_RIGHT = range(6)
 
@@ -32,6 +32,7 @@
 
 DERIV = lobatto_derivative()
 SECOND = DERIV @ DERIV
+HYPER = -step_size * hyper_coef
 
 
 def seam_table(length):
@@ -56,12 +57,13 @@
     first = np.kron(np.eye(length // 4), DERIV.T)
     second = first @ first
     seam = seam_table(length)
-    hyper = -step_size * hyper_coef
+    inner = (seam @ second) @ seam[:length]
+    inner[:, 0] += 0.5 * SECOND[3, 3] * seam[:, 0]
+    inner[:, length - 1] += 0.5 * SECOND[0, 0] * seam[:, length - 1]
+    last = np.concatenate([seam, HYPER * inner], axis=0)
     made = (
         np.concatenate([-step_size * first, second], axis=1),
-        np.concatenate([hyper * (seam @ second), seam], axis=1),
-        np.concatenate([-step_size * (seam @ first), seam @ second, seam], axis=1),
-        seam,
+        np.concatenate([-step_size * (last @ first), last @ second, last], axis=1),
     )
     return [m.astype(np.float32) for m in made]
 
@@ -72,9 +74,7 @@
         (m - h.astype(np.float32)).astype(jnp.bfloat16) for m, h in zip(tables(length), high)
     ]
     opening = np.concatenate([high[0], low[0]], axis=1)
-    rest = np.concatenate(
-        [high[1], low[1][:, :length], high[2], low[2][:, : 2 * length], high[3]], axis=1
-    )
+    rest = np.concatenate([high[1], low[1]], axis=1)
     return [jnp.asarray(opening), jnp.asarray(rest)]
 
 
@@ -112,9 +112,41 @@
     return out
 
 
+def outer_parts(base, lap):
+    n = len(lap)
+    m = [[float(HYPER * v) for v in line] for line in SECOND]
+    first = base[0] + m[0][1] * lap[1] + m[0][2] * lap[2]
+    first = first + (0.5 * m[0][3]) * (lap[3] + lap[4])
+    final = base[n - 1] + m[3][2] * lap[n - 2] + m[3][1] * lap[n - 3]
+    final = final + (0.5 * m[3][0]) * (lap[n - 4] + lap[n - 5])
+    return first, final
+
+
+def row_seam(rows, above, below):
+    n = len(rows)
+    done = list(rows)
+    for r in range(3, n - 1, 4):
+        done[r] = done[r + 1] = 0.5 * rows[r] + 0.5 * rows[r + 1]
+    done[0] = 0.5 * rows[0] + 0.5 * above
+    done[n - 1] = 0.5 * rows[n - 1] + 0.5 * below
+    return done
+
+
+def row_part(base, lap, above, below):
+    n = len(lap)
+    seamed = row_seam(lap, above[1], below[1])
+    bent = by_elements(lambda s: second_rows(s, HYPER), seamed)
+    ends = float(HYPER * SECOND[3, 3]), float(HYPER * SECOND[0, 0])
+    joint = row_seam(
+        [b + y for b, y in zip(base, bent)],
+        above[0] + ends[0] * seamed[0], below[0] + ends[1] * seamed[n - 1],
+    )
+    return joint, seamed
+
+
 def transport(
     sizes, tr_in, wind_in, shift_in, frac_in, opening_in, rest_in, out, field, wind, shift, frac,
-    opening, rest, moved_on, held, ahead, row_out, row_in, edge_out, edge_in,
+    opening, rest, moved_on, held, held_lap, row_out, row_in, edge_out, edge_in,
     row_send, row_recv, edge_send, edge_recv, tr_sem, in_sem,
 ):
     bins, levels, nr, nc = sizes
@@ -199,55 +231,64 @@
     def first_table(field):
         return times(field, opening, 0, 2 * nc, 2 * nc, 2 * nc)
 
-    def hyper_table(field):
-        return times(field, rest, 0, 2 * nc, 2 * nc, nc)
-
     def middle_table(field):
-        return times(field, rest, 3 * nc, 3 * nc, 6 * nc, 2 * nc)
+        return times(field, rest, 0, 3 * nc, 3 * nc, 3 * nc)
 
     def last_table(field):
-        return times(field, rest, 8 * nc, nc, 0, 0)[0]
-
-    def send(phase, chunk, rows):
+        return times(field, rest, 2 * nc, nc, 5 * nc, nc)[0]
+
+    def send(phase, chunk, base, lap):
         slot = phase * CHUNKS + chunk
-        row_out[slot, 0] = rows[0]
-        row_out[slot, 1] = rows[nr - 1]
+        ends = outer_parts(base, lap)
+        for side in range(2):
+            row_out[slot, side, 0] = ends[side]
+            row_out[slot, side, 1] = lap[side * (nr - 1)]
+        base_t, lap_t = flatten(base).T, flatten(lap).T
+        near = list(range(5)) + list(range(nc - 5, nc))
+        lap_lines = [lap_t[i : i + 1] for i in near]
+        base_lines = [base_t[i : i + 1] for i in near]
+        ends = outer_parts(base_lines, lap_lines)
+        for side in range(2):
+            edge_out[slot, side, 0] = ends[side]
+            edge_out[slot, side, 1] = lap_lines[side * (len(near) - 1)]
+        if COMM:
+            if phase == 0 and chunk == 0:
+                pl.semaphore_wait(barrier, len(partners))
+            for copy in copies(phase, chunk):
+                copy.start()
         for r in range(nr):
-            held[chunk, r] = rows[r]
-        turned = flatten(rows).T
-        edge_out[slot, 0] = turned[0:1]
-        edge_out[slot, 1] = turned[nc - 1 : nc]
-        if not COMM:
-            return
-        if phase == 0 and chunk == 0:
-            pl.semaphore_wait(barrier, len(partners))
-        for copy in copies(phase, chunk):
-            copy.start()
-
-    def row_seam(rows, above, below):
-        done = list(rows)
-        for r in range(3, nr - 1, 4):
-            done[r] = done[r + 1] = 0.5 * rows[r] + 0.5 * rows[r + 1]
-        done[0] = 0.5 * rows[0] + 0.5 * above
-        done[nr - 1] = 0.5 * rows[nr - 1] + 0.5 * below
-        return done
+            held[chunk, r] = base[r]
+            held_lap[chunk, r] = lap[r]
 
     def joined(phase, chunk):
         slot = phase * CHUNKS + chunk
         for copy in copies(phase, chunk) if COMM else ():
             copy.wait_recv()
-        rows = row_seam([held[chunk, r] for r in range(nr)], row_in[slot, 0], row_in[slot, 1])
-        lanes = jnp.concatenate(
-            [edge_in[slot, i] for i in range(6)] + [jnp.zeros((122, flat), jnp.float32)], axis=0
+        rows, row_laps = row_part(
+            [held[chunk, r] for r in range(nr)], [held_lap[chunk, r] for r in range(nr)],
+            (row_in[slot, 0, 0], row_in[slot, 0, 1]), (row_in[slot, 1, 0], row_in[slot, 1, 1]),
         )
-        edges = as_rows(lanes.T)
-        lane = lax.broadcasted_iota(jnp.int32, edges[0].shape, 2)
-        own = lane < 2
-        side = [jnp.where(own, e, 0.0) for e in edges]
-        from_up = jnp.where((lane >= 2) & (lane < 4), edges[nr - 1], 0.0)
-        from_down = jnp.where((lane >= 4) & (lane < 6), edges[0], 0.0)
-        side = row_seam(side, from_up, from_down)
-        return jnp.concatenate([flatten(rows), flatten(side)], axis=1)
+
+        def turned(kind):
+            lines = [edge_in[slot, i, kind] for i in range(6)]
+            blank = jnp.zeros((nc - 6, flat), jnp.float32)
+            return as_rows(jnp.concatenate(lines + [blank], axis=0).T)
+
+        base, lap = turned(0), turned(1)
+        lane = lax.broadcasted_iota(jnp.int32, base[0].shape, 2)
+        own, upper = lane < 2, (lane >= 2) & (lane < 4)
+        lower = (lane >= 4) & (lane < 6)
+        first, final = outer_parts(base, lap)
+
+        def only(mask, value):
+            return jnp.where(mask, value, 0.0)
+
+        side, side_laps = row_part(
+            [only(own, v) for v in base], [only(own, v) for v in lap],
+            (only(upper, final), only(upper, lap[nr - 1])),
+            (only(lower, first), only(lower, lap[0])),
+        )
+        return jnp.concatenate([flatten(v) for v in (rows, side, row_laps, side_laps)], axis=1)
 
     def wind_rows(chunk, which):
         return [
@@ -269,19 +310,16 @@
         slope_y = by_elements(lambda s: first_rows(s, -step_size), rows)
         second_y = by_elements(lambda s: second_rows(s, 1.0), rows)
         sx, lx = slope_x, second_x
-        laplace = []
+        base, lap = [], []
         for r in range(nr):
             moved = rows[r] + wx[r] * sx[r] + wy[r] * slope_y[r]
+            bent = lx[r] + second_y[r]
             if start is not None:
                 moved = scale * start[r] + scale * moved
-            ahead[chunk, r] = moved
-            laplace.append(lx[r] + second_y[r])
-        return laplace
-
-    def finish(chunk, made, scale):
-        hx, h = made
-        hy = by_elements(lambda s: second_rows(s, -step_size * hyper_coef), h)
-        return [ahead[chunk, r] + scale * (hx[r] + hy[r]) for r in range(nr)]
+                bent = scale * bent
+            base.append(moved)
+            lap.append(bent)
+        return base, lap
 
     def remap(weights, level):
         def at(b):
@@ -305,16 +343,12 @@
             loads[0].wait()
             loads[1].wait()
         rows = tracer_rows(chunk)
-        send(0, chunk, lead(chunk, rows, *first_table(flatten(rows)), None, 1.0))
+        send(0, chunk, *lead(chunk, rows, *first_table(flatten(rows)), None, 1.0))
     for load in loads[2:]:
         load.wait()
     for chunk in range(CHUNKS):
-        send(1, chunk, finish(chunk, hyper_table(joined(0, chunk)), 1.0))
-    for chunk in range(CHUNKS):
-        slope_x, second_x, rows = middle_table(joined(1, chunk))
-        send(2, chunk, lead(chunk, rows, slope_x, second_x, tracer_rows(chunk), 0.5))
-    for chunk in range(CHUNKS):
-        send(3, chunk, finish(chunk, hyper_table(joined(2, chunk)), 0.5))
+        slope_x, second_x, rows = middle_table(joined(0, chunk))
+        send(1, chunk, *lead(chunk, rows, slope_x, second_x, tracer_rows(chunk), 0.5))
     weights = []
     for k in range(5):
         weights.append(
@@ -322,7 +356,7 @@
             + jnp.where(shift[...] + 1 == k, frac[...], 0.0)
         )
     for chunk in range(CHUNKS):
-        rows = last_table(joined(3, chunk))
+        rows = last_table(joined(1, chunk))
         for l in range(step):
             level = chunk * step + l
             for r in range(nr):
@@ -356,10 +390,10 @@
             pltpu.VMEM((bins * levels * nr, nc), jnp.float32),
             pltpu.VMEM((CHUNKS, nr, step, bins, nc), jnp.float32),
             pltpu.VMEM((CHUNKS, nr, step, bins, nc), jnp.float32),
-            pltpu.VMEM((slots, 2, step, bins, nc), jnp.float32),
-            pltpu.VMEM((slots, 2, step, bins, nc), jnp.float32),
-            pltpu.VMEM((slots, 2, 1, flat), jnp.float32),
-            pltpu.VMEM((slots, 6, 1, flat), jnp.float32),
+            pltpu.VMEM((slots, 2, 2, step, bins, nc), jnp.float32),
+            pltpu.VMEM((slots, 2, 2, step, bins, nc), jnp.float32),
+            pltpu.VMEM((slots, 2, 2, 1, flat), jnp.float32),
+            pltpu.VMEM((slots, 6, 2, 1, flat), jnp.float32),
             pltpu.SemaphoreType.DMA((slots, 2)),
             pltpu.SemaphoreType.DMA((slots, 2)),
             pltpu.SemaphoreType.DMA((slots, 6)),

time: 32.9 us -> 28.7 us (0.87)
  Pallas kernels: 30.5 us -> 26.3 us
    pallas_call x1, Pallas kernels: 30.5 us -> 26.3 us  [body(): pl.pallas_call(functools.partial(transport, sizes), out_shape=jax.ShapeDt...]
where the time goes in v2:
time: 28.7 us; the launch traced here: 28.6 us
  Pallas kernels  26.3 us (92%)
  local copies, waits for them, and re-layouts  2.21 us (8%)
    pallas_call x1, Pallas kernels, body(): pl.pallas_call(functools.partial(transport, sizes), out_shape=jax.ShapeDt...  26.3 us
    unnamed x1, local copies, waits for them, and re-layouts  2.21 us

profile of v2, /device:TPU:0, one launch (start us, length us, event | category | flops | bytes accessed | tf_op | source)
XLA Modules:
  0.0 28.6 jit_solution(16281559547863343736)
XLA Ops:
  0.0 26.3 %transport.1 = f32[40,6,8,128]{3,2,1,0:T(8,128)} custom-call(f32[40,6,8,128]{3,2,1,0:T(8,128)} %tr_in.1, f32[2,6,8,128]{3,2,1,0:T(8,128)} %wind_in.1, s32[8,128]{1,0:T(8,128)} %shift_in.1, f32[8,128]{1,0:T(8,128)} %frac_in.1, bf16[128,512]{1,0:T(8,128)(2,1)} %constant.4.clone.opening_in, bf16[512,768]{1,0:T(8,128)(2,1)} %constant.5.clone.rest_in), custom_call_target="tpu_custom_call" | custom-call | tf_op jit(solution)/shard_map/transport/pallas_call | solution.py:378
  26.3 2.2 %copy.8 = f32[40,6,8,128]{3,2,1,0:T(8,128)} copy(f32[40,6,8,128]{3,2,1,0:T(8,128)} %transport.1) | data formatting | bytes 1966080

commit v3 on v2

--- a/solution.py
+++ b/solution.py
@@ -10,7 +10,7 @@
 step_size = 0.25
 hyper_coef = 0.001
 MESH = pl.DeviceIdType.MESH
-CHUNKS = 2
+CHUNKS = 3
 PHASES = 2
 COMM = True
 LEFT, RIGHT, UP_LEFT, UP_RIGHT, DOWN_LEFT, DOWN_RIGHT = range(6)

time: 28.7 us -> 29.1 us (1.014)
  Pallas kernels: 26.3 us -> 26.7 us
    pallas_call x1, Pallas kernels: 26.3 us -> 26.7 us  [body(): pl.pallas_call(functools.partial(transport, sizes), out_shape=jax.ShapeDt...]
where the time goes in v3:
time: 29.1 us; the launch traced here: 28.9 us
  Pallas kernels  26.7 us (92%)
  local copies, waits for them, and re-layouts  2.21 us (8%)
    pallas_call x1, Pallas kernels, body(): pl.pallas_call(functools.partial(transport, sizes), out_shape=jax.ShapeDt...  26.7 us
    unnamed x1, local copies, waits for them, and re-layouts  2.21 us

profile of v3, /device:TPU:0, one launch (start us, length us, event | category | flops | bytes accessed | tf_op | source)
XLA Modules:
  0.0 28.9 jit_solution(10138032155488095043)
XLA Ops:
  0.0 26.7 %transport.1 = f32[40,6,8,128]{3,2,1,0:T(8,128)} custom-call(f32[40,6,8,128]{3,2,1,0:T(8,128)} %tr_in.1, f32[2,6,8,128]{3,2,1,0:T(8,128)} %wind_in.1, s32[8,128]{1,0:T(8,128)} %shift_in.1, f32[8,128]{1,0:T(8,128)} %frac_in.1, bf16[128,512]{1,0:T(8,128)(2,1)} %constant.4.clone.opening_in, bf16[512,768]{1,0:T(8,128)(2,1)} %constant.5.clone.rest_in), custom_call_target="tpu_custom_call" | custom-call | tf_op jit(solution)/shard_map/transport/pallas_call | solution.py:378
  26.7 2.2 %copy.8 = f32[40,6,8,128]{3,2,1,0:T(8,128)} copy(f32[40,6,8,128]{3,2,1,0:T(8,128)} %transport.1) | data formatting | bytes 1966080
